TPU v7x, 32 devices: a whole 2x2x4 slice. The times are simulated.
32 devices in a mesh: dp: 8 (over z, x), tensor: 4 (over y, core).
Axes of the slice: x: 2, y: 2, z: 4, core: 2. Of those that a mesh axis runs over, the one named last changes fastest.
Arguments:
- tokens: bfloat16 [32768, 768], P('dp'), may hold values from -6 to 6
- cotangent: bfloat16 [32768, 768], P('dp'), may hold values from -6 to 6
- short_len: int32 [128], P('dp'), may hold values from 64 to 128, as said below
- long_len: int32 [32], P('dp'), may hold values from 256 to 512, as said below
- short_count: int32 [8], P('dp'), may hold values from 8 to 16, as said below
- long_count: int32 [8], P('dp'), may hold values from 0 to 4, as said below
- query_weight: bfloat16 [768, 768], P(None, 'tensor'), may hold values from -0.3125 to 0.3125
- query_bias: bfloat16 [768], P('tensor'), may hold values from -3 to 3
- key_weight: bfloat16 [768, 768], P(None, 'tensor'), may hold values from -0.3125 to 0.3125
- value_weight: bfloat16 [768, 768], P(None, 'tensor'), may hold values from -0.21875 to 0.21875
- value_bias: bfloat16 [768], P('tensor'), may hold values from -3 to 3
- output_weight: bfloat16 [768, 768], P('tensor'), may hold values from -0.875 to 0.875
- output_bias: bfloat16 [768], replicated, may hold values from -3 to 3
- first_gain: bfloat16 [768], replicated, may hold values from 0.5 to 1.5
- first_shift: bfloat16 [768], replicated, may hold values from -3 to 3
- up_weight: bfloat16 [768, 3072], P(None, 'tensor'), may hold values from -0.21875 to 0.21875
- up_bias: bfloat16 [3072], P('tensor'), may hold values from -3 to 3
- down_weight: bfloat16 [3072, 768], P('tensor'), may hold values from -0.109375 to 0.109375
- down_bias: bfloat16 [768], replicated, may hold values from -2 to 2
- second_gain: bfloat16 [768], replicated, may hold values from 0.5 to 1.5
- second_shift: bfloat16 [768], replicated, may hold values from -3 to 3
Outputs:
- layer_output: bfloat16 [32768, 768], P('dp')
- input_grad: float32 [32768, 768], P('dp')
- grad_query_weight: float32 [768, 768], P(None, 'tensor')
- grad_query_bias: float32 [768], P('tensor')
- grad_key_weight: float32 [768, 768], P(None, 'tensor')
- grad_value_weight: float32 [768, 768], P(None, 'tensor')
- grad_value_bias: float32 [768], P('tensor')
- grad_output_weight: float32 [768, 768], P('tensor')
- grad_output_bias: float32 [768], replicated
- grad_first_gain: float32 [768], replicated
- grad_first_shift: float32 [768], replicated
- grad_up_weight: float32 [768, 3072], P(None, 'tensor')
- grad_up_bias: float32 [3072], P('tensor')
- grad_down_weight: float32 [3072, 768], P('tensor')
- grad_down_bias: float32 [768], replicated
- grad_second_gain: float32 [768], replicated
- grad_second_shift: float32 [768], replicated
Inputs may be any that keep to these rules, and one draw needn't show every extreme that they name: `short_len`: some slot has exactly 128 valid tokens. `long_len`: some slot has exactly 512 valid tokens. `short_count`: slots at or beyond the count hold no valid tokens; some index of dp has all 16 live. `long_count`: slots at or beyond the count hold no valid tokens; some index of dp has all 4 live.
All inputs are finite; a program needn't handle non-finite values.
Results may differ from a plain program's by a relative error of at most 0.02.
Values may be sent and summed in bfloat16 or wider, within the bound.
No kernel may reach another device: no remote copies, remote signals or barrier semaphores. Data moves between devices by JAX's collectives and lax.ppermute only.
A program may use at most 256 MiB of HBM per device.

v0:
```python
import jax
import jax.numpy as jnp
from jax import lax
from jax.sharding import PartitionSpec as P

HEAD_DIM = 64
SHORT_LEN = 128
LONG_LEN = 512


def token_masks(lengths, live_count, slot_count, slot_width):
    position = jnp.arange(slot_width, dtype=jnp.int32)
    live_slots = jnp.arange(slot_count, dtype=jnp.int32) < live_count
    return (position[None, :] < lengths[:, None]) & live_slots[:, None]


def row_dot(left_side, right_side):
    return jnp.dot(left_side, right_side, preferred_element_type=jnp.float32)


def dot_first(left_side, right_side):
    return lax.dot_general(
        left_side, right_side, (((0,), (0,)), ((), ())), preferred_element_type=jnp.float32
    )


def dot_last(left_side, right_side):
    return lax.dot_general(
        left_side, right_side, (((1,), (1,)), ((), ())), preferred_element_type=jnp.float32
    )


def norm_forward(values, norm_gain, norm_shift):
    centre = values - jnp.mean(values, axis=-1, keepdims=True)
    scale_rows = lax.rsqrt(jnp.mean(centre * centre, axis=-1, keepdims=True) + 1e-12)
    normed = centre * scale_rows
    return (normed * norm_gain + norm_shift, normed, scale_rows)


def norm_backward(incoming, normed, scale_rows, norm_gain):
    grad_normed = incoming * norm_gain
    inner_terms = grad_normed - jnp.mean(grad_normed, axis=-1, keepdims=True)
    inner_terms = inner_terms - normed * jnp.mean(grad_normed * normed, axis=-1, keepdims=True)
    return (scale_rows * inner_terms, jnp.sum(incoming * normed, axis=0), jnp.sum(incoming, axis=0))


def gelu_slope(up_inner):
    normal_cdf = 0.5 * (1.0 + lax.erf(up_inner * 0.7071067811865476))
    return normal_cdf + up_inner * jnp.exp(-0.5 * up_inner * up_inner) * 0.3989422804014327


def scores_of(queries, key_states, valid_keys, scale_factor):
    raw_scores = (
        jnp.einsum("bqhe,bkhe->bhqk", queries, key_states, preferred_element_type=jnp.float32)
        * scale_factor
    )
    return jnp.where(valid_keys[:, None, None, :], raw_scores, -30000.0)


def attend(queries, key_states, value_states, valid_keys, scale_factor):
    scores = scores_of(queries, key_states, valid_keys, scale_factor)
    row_top = jnp.max(scores, axis=-1, keepdims=True)
    row_total = jnp.sum(jnp.exp(scores - row_top), axis=-1, keepdims=True)
    logsum = row_top + jnp.log(row_total)
    probs_low = jnp.exp(scores - logsum).astype(jnp.bfloat16)
    mixed_heads = jnp.einsum(
        "bhqk,bkhe->bqhe", probs_low, value_states, preferred_element_type=jnp.float32
    )
    return (mixed_heads.astype(jnp.bfloat16), logsum)


def attend_back(queries, key_states, value_states, valid_keys, scale_factor, logsum, grad_mixed):
    scores = scores_of(queries, key_states, valid_keys, scale_factor)
    probs = jnp.exp(scores - logsum)
    grad_probs = jnp.einsum(
        "bqhe,bkhe->bhqk", grad_mixed, value_states, preferred_element_type=jnp.float32
    )
    grad_scores = probs * (grad_probs - jnp.sum(probs * grad_probs, axis=-1, keepdims=True))
    grad_scores = jnp.where(valid_keys[:, None, None, :], grad_scores, 0.0).astype(jnp.bfloat16)
    grad_queries = (
        jnp.einsum("bhqk,bkhe->bqhe", grad_scores, key_states, preferred_element_type=jnp.float32)
        * scale_factor
    )
    grad_keys = (
        jnp.einsum("bhqk,bqhe->bkhe", grad_scores, queries, preferred_element_type=jnp.float32)
        * scale_factor
    )
    grad_values = jnp.einsum(
        "bhqk,bqhe->bkhe",
        probs.astype(jnp.bfloat16),
        grad_mixed,
        preferred_element_type=jnp.float32,
    )
    return (grad_queries, grad_keys, grad_values)


def per_device(
    tokens,
    cotangent,
    short_len,
    long_len,
    short_count,
    long_count,
    query_weight,
    query_bias,
    key_weight,
    value_weight,
    value_bias,
    output_weight,
    output_bias,
    first_gain,
    first_shift,
    up_weight,
    up_bias,
    down_weight,
    down_bias,
    second_gain,
    second_shift,
):
    short_slots = short_len.shape[0]
    long_slots = long_len.shape[0]
    short_rows = short_slots * SHORT_LEN
    head_width = query_weight.shape[1]
    heads_here = head_width // HEAD_DIM
    scale_factor = HEAD_DIM ** (-0.5)
    short_valid = token_masks(short_len, short_count[0], short_slots, SHORT_LEN)
    long_valid = token_masks(long_len, long_count[0], long_slots, LONG_LEN)
    valid_rows = jnp.concatenate([short_valid.reshape(-1), long_valid.reshape(-1)]).astype(
        jnp.float32
    )

    def short_view(flat_rows):
        return flat_rows[:short_rows].reshape(short_slots, SHORT_LEN, heads_here, HEAD_DIM)

    def long_view(flat_rows):
        return flat_rows[short_rows:].reshape(long_slots, LONG_LEN, heads_here, HEAD_DIM)

    queries = (row_dot(tokens, query_weight) + query_bias).astype(jnp.bfloat16)
    key_states = row_dot(tokens, key_weight).astype(jnp.bfloat16)
    value_states = (row_dot(tokens, value_weight) + value_bias).astype(jnp.bfloat16)
    mixed_short, logsum_short = attend(
        short_view(queries),
        short_view(key_states),
        short_view(value_states),
        short_valid,
        scale_factor,
    )
    flat_short = mixed_short.reshape(short_rows, head_width)
    mixed_long, logsum_long = attend(
        long_view(queries), long_view(key_states), long_view(value_states), long_valid, scale_factor
    )
    flat_long = mixed_long.reshape(long_slots * LONG_LEN, head_width)
    mixed_heads = jnp.concatenate([flat_short, flat_long], axis=0)
    attn_sum = lax.psum(row_dot(mixed_heads, output_weight).astype(jnp.bfloat16), "tensor").astype(
        jnp.float32
    )
    hidden = tokens.astype(jnp.float32) + (attn_sum + output_bias)
    first_norm, normed_one, scale_one = norm_forward(hidden, first_gain, first_shift)
    first_low = first_norm.astype(jnp.bfloat16)
    up_inner = row_dot(first_low, up_weight) + up_bias
    active = jax.nn.gelu(up_inner, approximate=False).astype(jnp.bfloat16)
    ffn_total = lax.psum(row_dot(active, down_weight).astype(jnp.bfloat16), "tensor").astype(
        jnp.float32
    )
    second_input = first_norm + (ffn_total + down_bias)
    second_norm, normed_two, scale_two = norm_forward(second_input, second_gain, second_shift)
    layer_output = second_norm.astype(jnp.bfloat16)
    upstream = cotangent.astype(jnp.float32) * valid_rows[:, None]
    grad_second_input, grad_second_gain, grad_second_shift = norm_backward(
        upstream, normed_two, scale_two, second_gain
    )
    grad_down_bias = jnp.sum(grad_second_input, axis=0)
    grad_ffn = grad_second_input.astype(jnp.bfloat16)
    grad_down_weight = dot_first(active, grad_ffn)
    grad_inner = dot_last(grad_ffn, down_weight) * gelu_slope(up_inner)
    grad_up_bias = jnp.sum(grad_inner, axis=0)
    grad_inner_low = grad_inner.astype(jnp.bfloat16)
    grad_up_weight = dot_first(first_low, grad_inner_low)
    back_total = lax.psum(
        dot_last(grad_inner_low, up_weight).astype(jnp.bfloat16), "tensor"
    ).astype(jnp.float32)
    grad_first = grad_second_input + back_total
    grad_hidden, grad_first_gain, grad_first_shift = norm_backward(
        grad_first, normed_one, scale_one, first_gain
    )
    grad_output_bias = jnp.sum(grad_hidden, axis=0)
    grad_attn = grad_hidden.astype(jnp.bfloat16)
    grad_output_weight = dot_first(mixed_heads, grad_attn)
    grad_mixed = dot_last(grad_attn, output_weight).astype(jnp.bfloat16)

    def bucket_back(view, valid_keys, logsum):
        grad_parts = attend_back(
            view(queries),
            view(key_states),
            view(value_states),
            valid_keys,
            scale_factor,
            logsum,
            view(grad_mixed),
        )
        row_count = grad_parts[0].shape[0] * grad_parts[0].shape[1]
        full_parts = tuple((piece.reshape(row_count, head_width) for piece in grad_parts))
        low_parts = tuple((piece.astype(jnp.bfloat16) for piece in full_parts))
        return (full_parts, low_parts)

    long_full, long_low = bucket_back(long_view, long_valid, logsum_long)
    short_full, short_low = bucket_back(short_view, short_valid, logsum_short)
    full_parts = tuple(
        (
            jnp.concatenate([first_piece, second_piece], axis=0)
            for first_piece, second_piece in zip(short_full, long_full)
        )
    )
    low_parts = tuple(
        (
            jnp.concatenate([first_piece, second_piece], axis=0)
            for first_piece, second_piece in zip(short_low, long_low)
        )
    )
    input_total = lax.psum(
        (
            dot_last(low_parts[0], query_weight)
            + dot_last(low_parts[1], key_weight)
            + dot_last(low_parts[2], value_weight)
        ).astype(jnp.bfloat16),
        "tensor",
    ).astype(jnp.float32)
    input_grad = grad_hidden + input_total
    grad_query_bias = jnp.sum(full_parts[0], axis=0)
    grad_value_bias = jnp.sum(full_parts[2], axis=0)
    grad_query_weight = dot_first(tokens, low_parts[0])
    grad_key_weight = dot_first(tokens, low_parts[1])
    grad_value_weight = dot_first(tokens, low_parts[2])
    summed_grads = (
        lax.psum(grad_query_weight.astype(jnp.bfloat16), "dp").astype(jnp.float32),
        lax.psum(grad_query_bias.astype(jnp.bfloat16), "dp").astype(jnp.float32),
        lax.psum(grad_key_weight.astype(jnp.bfloat16), "dp").astype(jnp.float32),
        lax.psum(grad_value_weight.astype(jnp.bfloat16), "dp").astype(jnp.float32),
        lax.psum(grad_value_bias.astype(jnp.bfloat16), "dp").astype(jnp.float32),
        lax.psum(grad_output_weight.astype(jnp.bfloat16), "dp").astype(jnp.float32),
        lax.psum(grad_output_bias.astype(jnp.bfloat16), "dp").astype(jnp.float32),
        lax.psum(grad_first_gain.astype(jnp.bfloat16), "dp").astype(jnp.float32),
        lax.psum(grad_first_shift.astype(jnp.bfloat16), "dp").astype(jnp.float32),
        lax.psum(grad_up_weight.astype(jnp.bfloat16), "dp").astype(jnp.float32),
        lax.psum(grad_up_bias.astype(jnp.bfloat16), "dp").astype(jnp.float32),
        lax.psum(grad_down_weight.astype(jnp.bfloat16), "dp").astype(jnp.float32),
        lax.psum(grad_down_bias.astype(jnp.bfloat16), "dp").astype(jnp.float32),
        lax.psum(grad_second_gain.astype(jnp.bfloat16), "dp").astype(jnp.float32),
        lax.psum(grad_second_shift.astype(jnp.bfloat16), "dp").astype(jnp.float32),
    )
    (
        grad_query_weight,
        grad_query_bias,
        grad_key_weight,
        grad_value_weight,
        grad_value_bias,
        grad_output_weight,
        grad_output_bias,
        grad_first_gain,
        grad_first_shift,
        grad_up_weight,
        grad_up_bias,
        grad_down_weight,
        grad_down_bias,
        grad_second_gain,
        grad_second_shift,
    ) = summed_grads
    return (
        layer_output,
        input_grad,
        grad_query_weight,
        grad_query_bias,
        grad_key_weight,
        grad_value_weight,
        grad_value_bias,
        grad_output_weight,
        grad_output_bias,
        grad_first_gain,
        grad_first_shift,
        grad_up_weight,
        grad_up_bias,
        grad_down_weight,
        grad_down_bias,
        grad_second_gain,
        grad_second_shift,
    )


def solution(mesh):
    return jax.shard_map(
        per_device,
        mesh=mesh,
        in_specs=(
            P("dp", None),
            P("dp", None),
            P("dp"),
            P("dp"),
            P("dp"),
            P("dp"),
            P(None, "tensor"),
            P("tensor"),
            P(None, "tensor"),
            P(None, "tensor"),
            P("tensor"),
            P("tensor", None),
            P(),
            P(),
            P(),
            P(None, "tensor"),
            P("tensor"),
            P("tensor", None),
            P(),
            P(),
            P(),
        ),
        out_specs=(
            P("dp", None),
            P("dp", None),
            P(None, "tensor"),
            P("tensor"),
            P(None, "tensor"),
            P(None, "tensor"),
            P("tensor"),
            P("tensor", None),
            P(),
            P(),
            P(),
            P(None, "tensor"),
            P("tensor"),
            P("tensor", None),
            P(),
            P(),
            P(),
        ),
        check_vma=False,
    )
```

profile of v0, /device:TPU:0, one launch (start us, length us, event | category | flops | bytes accessed | tf_op | source)
XLA Modules:
  0.0 969.7 jit_solution(17946246277438331448)
XLA Ops:
  10.5 5.0 fusion.51
  17.3 5.0 fusion.52
  23.4 2.8 reshape.265
  27.3 5.0 convolution_convert_fusion.4
  33.5 2.3 reshape.266
  38.2 2.3 fusion.65
  44.5 3.0 fusion.22
  47.6 3.5 exponential_reduce_fusion
  51.2 3.2 fusion.94
  56.5 4.6 convolution_convert_fusion
  61.2 122.3 %all-reduce.8.cloned.1.call-done = bf16[4096,768]{1,0:T(8,128)(2,1)} async-done(((bf16[4096,768]{1,0:T(8,128)(2,1)}), bf16[4096,768]{1,0:T(8,128)(2,1)}) %all-reduce.8.cloned.1.call-update) | async-done | bytes 6291472 | tf_op jit(solution)/shard_map/psum | solution.py:154
  183.5 6.9 fusion.23
  190.4 5.7 multiply_reduce_fusion.6
  196.2 35.1 %fusion.4 = (bf16[4096,768]{1,0:T(8,128)(2,1)S(1)}, f32[4096,768]{1,0:T(8,128)}) fusion(f32[768]{0:T(1024)S(1)} %convert_element_type.287, bf16[768,768]{1,0:T(8,128)(2,1)S(1)} %copy-done, f32[768]{0:T(1024)S(1)} %convert_element_type.285, f32[768]{0:T(1024)S(1)} %convert_element_type.284, f32[4096]{0:T(1024)S(1)} %add_rsqrt_fusion.1, ...), kind=kOutput, calls=%fused_computation.6 | convolution fusion | flops 5067767808 | bytes 32681984 | tf_op jit(solution)/shard_map/dot_general | solution.py:18
  231.3 2.6 copy-done.56
  233.9 7.0 convolution_convert_fusion.2
  241.2 119.7 %all-reduce.10.cloned.1.call-done = bf16[4096,768]{1,0:T(8,128)(2,1)} async-done(((bf16[4096,768]{1,0:T(8,128)(2,1)}), bf16[4096,768]{1,0:T(8,128)(2,1)}) %all-reduce.10.cloned.1.call-update) | async-done | bytes 6291472 | tf_op jit(solution)/shard_map/psum | solution.py:162
  360.9 9.4 fusion.168
  371.8 8.3 multiply_reduce_fusion
  380.1 7.3 subtract_multiply_fusion.1
  387.5 13.6 %fusion.177 = (bf16[768]{0:T(1024)(128)(2,1)}, bf16[4096,768]{1,0:T(8,128)(2,1)S(1)}) fusion(f32[4096,768]{1,0:T(8,128)} %get-tuple-element.62, f32[768]{0:T(1024)S(1)} %convert_element_type.287, bf16[768,768]{1,0:T(8,128)(2,1)S(1)} %copy-done.55, f32[4096,768]{1,0:T(8,128)} %get-tuple-element.45), kind=kOutput, calls=%fused_computation.211 | convolution fusion | flops 4872731648 | bytes 32641536 | tf_op jit(solution)/shard_map/dot_general | solution.py:28
  401.0 2.6 copy-done.57
  403.6 7.0 convolution_convert_fusion.1
  411.1 15.0 %fusion.82 = bf16[768,768]{1,0:T(8,128)(2,1)} fusion(bf16[4096,768]{1,0:T(8,128)(2,1)} %copy-done.57, f32[768]{0:T(1024)S(1)} %convert_element_type.285, f32[768]{0:T(1024)S(1)} %convert_element_type.284, bf16[4096,768]{1,0:T(8,128)(2,1)} %all-reduce.8.cloned.1.call-done, bf16[4096,768]{1,0:T(8,128)(2,1)} %param.21, f32[4096]{0:T(1024)S(1)} %add_rsqrt_fusion.1, ...), kind=kOutput, calls=%fused_computation.114 | convolution fusion | flops 4860739584 | bytes 20096000 | tf_op jit(solution)/shard_map/dot_general | solution.py:22
  426.1 104.5 %all-reduce.12.cloned.1.call-done = bf16[4096,768]{1,0:T(8,128)(2,1)} async-done(((bf16[4096,768]{1,0:T(8,128)(2,1)}), bf16[4096,768]{1,0:T(8,128)(2,1)}) %all-reduce.12.cloned.1.call-update) | async-done | bytes 6291472 | tf_op jit(solution)/shard_map/psum | solution.py:179
  530.5 13.8 %multiply_reduce_fusion.1 = (bf16[768]{0:T(1024)(128)(2,1)S(1)}, f32[4096]{0:T(1024)S(1)}, f32[4096]{0:T(1024)S(1)}, bf16[768]{0:T(1024)(128)(2,1)S(1)}, bf16[768]{0:T(1024)(128)(2,1)S(1)}) fusion(f32[4096,768]{1,0:T(8,128)} %get-tuple-element.45, bf16[4096,768]{1,0:T(8,128)(2,1)} %all-reduce.12.cloned.1.call-done, f32[4096]{0:T(1024)S(1)} %add_rsqrt_fusion.1, ...), kind=kLoop, calls=%fused_computation.13 | loop fusion | flops 50321152 | bytes 31533568 | tf_op jit(solution)/shard_map/reduce_sum | solution.py:44
  544.4 9.6 fusion.167
  559.5 2.4 fusion.115
  562.0 7.9 fusion.98
  569.9 8.0 bitcast_convert_fusion.3
  577.9 4.0 bitcast_convert_fusion.1
  581.9 2.3 reshape.269
  585.1 7.5 bitcast_convert_fusion
  592.6 7.6 fusion.111
  600.2 23.5 %fusion.95 = bf16[4,512,3,64]{1,3,2,0:T(8,128)(2,1)} fusion(f32[4,3,512,512]{2,3,1,0:T(8,128)} %fusion.111, f32[4,3,512,512]{2,3,1,0:T(8,128)} %copy-done.4, f32[4,3,512]{2,1,0:T(4,128)S(1)} %copy-done.39, pred[4,512]{1,0:T(4,128)(4,1)S(1)} %copy-done.37, bf16[4,512,3,64]{1,0,3,2:T(4,128)(2,1)S(1)} %copy-done.18), kind=kOutput, calls=%fused_computation.119 | convolution fusion | flops 438049280 | bytes 26765312 | tf_op jit(solution)/shard_map/bhqk,bqhe->bkhe/dot_general | solution.py:85
  623.7 23.8 %bitcast_convert_fusion.2 = (bf16[4,512,3,64]{1,3,2,0:T(8,128)(2,1)}, f32[4,3,64,512]{3,2,1,0:T(8,128)}) fusion(f32[4,3,512,512]{2,3,1,0:T(8,128)} %fusion.111, f32[4,3,512,512]{2,3,1,0:T(8,128)} %copy-done.4, f32[4,3,512]{2,1,0:T(4,128)S(1)} %copy-done.39, pred[4,512]{1,0:T(4,128)(4,1)S(1)} %copy-done.37, bf16[4,512,3,64]{1,0,3,2:T(4,128)(2,1)S(1)} %copy-done.20), kind=kOutput, calls=%fused_computation.104 | convolution fusion | flops 438049280 | bytes 28338176 | tf_op jit(solution)/shard_map/bhqk,bkhe->bqhe/dot_general | solution.py:81
  655.6 6.4 fusion.178
  663.1 6.5 fusion.179
  670.8 12.8 %add_convert_fusion = bf16[4096,768]{1,0:T(8,128)(2,1)} fusion(f32[4096,768]{1,0:T(8,128)} %fusion.178, f32[4096,768]{1,0:T(8,128)} %fusion.179, bf16[4096,192]{0,1:T(8,128)(2,1)S(1)} %constant_dynamic-update-slice_fusion.3, bf16[768,192]{0,1:T(8,128)(2,1)S(1)} %copy-done.31), kind=kOutput, calls=%fused_computation.15 | convolution fusion | flops 1217396736 | bytes 33325056 | tf_op jit(solution)/shard_map/dot_general | solution.py:28
  683.7 12.1 %fusion.79 = bf16[768,768]{1,0:T(8,128)(2,1)} fusion(bf16[4096,768]{1,0:T(8,128)(2,1)} %copy-done.56, f32[4096,768]{1,0:T(8,128)} %get-tuple-element.45), kind=kOutput, calls=%fused_computation.113 | convolution fusion | flops 4835573760 | bytes 20054016 | tf_op jit(solution)/shard_map/dot_general | solution.py:22
  695.8 5.2 fusion.107
  701.1 5.1 fusion.106
  716.6 36.9 %all-reduce = (bf16[192]{0:T(256)(128)(2,1)S(1)}, bf16[192]{0:T(256)(128)(2,1)S(1)}, bf16[768]{0:T(1024)(128)(2,1)S(1)}, bf16[768]{0:T(1024)(128)(2,1)S(1)}, bf1...) all-reduce(bf16[192]{0:T(256)(128)(2,1)S(1)} %convert_element_type., ...), channel_id=1, replica_groups=mesh['dp'=8,'tensor'=4] {'dp'}, use_global_device_ids=true, to_apply=%region_21.22 | all-reduce | flops 5760 | bytes 23040 | tf_op jit(solution)/shard_map/psum | solution.py:236
  758.8 44.8 %all-reduce.14.cloned.1.call-done = bf16[4096,768]{1,0:T(8,128)(2,1)} async-done(((bf16[4096,768]{1,0:T(8,128)(2,1)}), bf16[4096,768]{1,0:T(8,128)(2,1)}) %all-reduce.14.cloned.1.call-update) | async-done | bytes 6291472 | tf_op jit(solution)/shard_map/psum | solution.py:220
  803.6 12.7 %convert_add_fusion = f32[4096,768]{1,0:T(8,128)} fusion(f32[4096,768]{1,0:T(8,128)} %copy-done.2, bf16[4096,768]{1,0:T(8,128)(2,1)} %all-reduce.14.cloned.1.call-done), kind=kLoop, calls=%fused_computation.14 | loop fusion | flops 6291456 | bytes 31457280 | tf_op jit(solution)/shard_map/add | solution.py:228
  816.2 133.8 %all-reduce.16.cloned.1.call-done = (bf16[768,192]{0,1:T(8,128)(2,1)}, bf16[768,192]{0,1:T(8,128)(2,1)}, bf16[768,192]{0,1:T(8,128)(2,1)}, bf16[192,768]{1,0:T(8...) async-done(((bf16[768,192]{0,1:T(8,128)(2,1)}, bf16[768,192]{0,1:T(8,128)(2,1)}, bf16[768,192]{0,1:T(8,128)(2,1)}, bf16[192,768]{1,0:T(8,128)(2,1)}, ...) | async-done | bytes 3538960 | tf_op jit(solution)/shard_map/psum | solution.py:235
  957.3 2.8 convert_element_type.345
  960.1 2.8 convert_element_type.349
  (227 shorter events, 57.4 us)
Async XLA Ops:
  7.2 188.9 %copy-start = (bf16[768,768]{1,0:T(8,128)(2,1)S(1)}, bf16[768,768]{1,0:T(8,128)(2,1)}, u32[]{:S(2)}) copy-start(bf16[768,768]{1,0:T(8,128)(2,1)} %param.36) | copy-start | bytes 3538948
  7.2 176.3 %all-reduce.8.cloned.1.call-start = ((), (), s32[]{:S(2)}) async-start(), calls=%async_computation | async-start | bytes 12582912 | tf_op jit(solution)/shard_map/psum | solution.py:154
  16.2 34.9 %copy-start.15 = (bf16[4,512,3,64]{1,0,3,2:T(4,128)(2,1)}, bf16[4,512,3,64]{1,0,3,2:T(4,128)(2,1)S(1)}, u32[]{:S(2)}) copy-start(bf16[4,512,3,64]{1,0,3,2:T(4,128)(2,1)S(1)} %reshape.264) | copy-start | bytes 2359300
  22.3 15.1 %copy-start.53 = (s32[16]{0:T(128)S(1)}, s32[16]{0:T(128)}, u32[]{:S(2)}) copy-start(s32[16]{0:T(128)} %param.23) | copy-start | bytes 196
  26.2 18.3 %copy-start.17 = (bf16[4,512,3,64]{1,0,3,2:T(4,128)(2,1)}, bf16[4,512,3,64]{1,0,3,2:T(4,128)(2,1)S(1)}, u32[]{:S(2)}) copy-start(bf16[4,512,3,64]{1,0,3,2:T(4,128)(2,1)S(1)} %reshape.265) | copy-start | bytes 2359300
  32.3 12.2 %copy-start.52 = (s32[4]{0:T(128)S(1)}, s32[4]{0:T(128)}, u32[]{:S(2)}) copy-start(s32[4]{0:T(128)} %param.24) | copy-start | bytes 52
  35.8 11.8 %copy-start.19 = (bf16[4,512,3,64]{1,0,3,2:T(4,128)(2,1)}, bf16[4,512,3,64]{1,0,3,2:T(4,128)(2,1)S(1)}, u32[]{:S(2)}) copy-start(bf16[4,512,3,64]{1,0,3,2:T(4,128)(2,1)S(1)} %reshape.266) | copy-start | bytes 2359300
  37.4 7.0 copy-start.27
  61.1 299.9 %all-reduce.10.cloned.1.call-start = ((), (), s32[]{:S(2)}) async-start(), calls=%async_computation.1 | async-start | bytes 12582912 | tf_op jit(solution)/shard_map/psum | solution.py:162
  61.2 134.9 %slice-start.3 = ((s8[6291456]{0:T(1024)(128)(4,1)}), s8[2097152]{0:T(1024)(128)(4,1)S(1)}, s32[]{:S(2)}) async-start(s8[6291456]{0:T(1024)(128)(4,1)} %bitcast.143), calls=%async_computation.8 | async-start | bytes 4194304
  183.5 6.9 copy-start.3
  196.2 37.8 %copy-start.54 = (bf16[768,768]{1,0:T(8,128)(2,1)S(1)}, bf16[768,768]{1,0:T(8,128)(2,1)}, u32[]{:S(2)}) copy-start(bf16[768,768]{1,0:T(8,128)(2,1)} %param.38) | copy-start | bytes 3538948
  233.9 7.2 copy-start.48
  233.9 7.2 copy-start.49
  233.9 7.2 copy-start.50
  241.0 289.5 %all-reduce.12.cloned.1.call-start = ((), (), s32[]{:S(2)}) async-start(), calls=%async_computation.2 | async-start | bytes 12582912 | tf_op jit(solution)/shard_map/psum | solution.py:179
  371.8 8.3 slice-start.7
  371.8 8.3 slice-start.8
  380.1 7.3 copy-start.55
  410.6 393.0 %all-reduce.14.cloned.1.call-start = ((), (), s32[]{:S(2)}) async-start(), calls=%async_computation.3 | async-start | bytes 12582912 | tf_op jit(solution)/shard_map/psum | solution.py:220
  530.5 13.9 %copy-start.5 = (bf16[4096,768]{1,0:T(8,128)(2,1)S(1)}, bf16[4096,768]{1,0:T(8,128)(2,1)}, u32[]{:S(2)}) copy-start(bf16[4096,768]{1,0:T(8,128)(2,1)} %all-reduce.12.cloned.1.call-done) | copy-start | bytes 18874372
  544.4 9.6 copy-start.25
  554.1 7.9 copy-start.26
  554.1 7.9 copy-start.35
  554.1 7.8 copy-start.41
  556.4 13.5 %copy-start.28 = (bf16[24,8,16,128]{3,2,1,0:T(8,128)(2,1)S(1)}, bf16[24,8,16,128]{3,2,1,0:T(8,128)(2,1)}, u32[]{:S(2)}) copy-start(bf16[24,8,16,128]{3,2,1,0:T(8,128)(2,1)} %copy-done.27) | copy-start | bytes 2359300
  562.0 23.1 %copy-start.37 = (pred[4,512]{1,0:T(4,128)(4,1)S(1)}, pred[4,512]{1,0:T(4,128)(4,1)}, u32[]{:S(2)}) copy-start(pred[4,512]{1,0:T(4,128)(4,1)} %copy-done.36) | copy-start | bytes 6148
  562.0 23.1 %copy-start.39 = (f32[4,3,512]{2,1,0:T(4,128)S(1)}, f32[4,3,512]{2,1,0:T(4,128)}, u32[]{:S(2)}) copy-start(f32[4,3,512]{2,1,0:T(4,128)} %copy-done.38) | copy-start | bytes 73732
  585.1 7.5 copy-start.16
  592.5 7.7 copy-start.18
  600.2 23.5 %copy-start.20 = (bf16[4,512,3,64]{1,0,3,2:T(4,128)(2,1)S(1)}, bf16[4,512,3,64]{1,0,3,2:T(4,128)(2,1)}, u32[]{:S(2)}) copy-start(bf16[4,512,3,64]{1,0,3,2:T(4,128)(2,1)} %copy-done.19) | copy-start | bytes 2359300
  623.7 23.9 %copy-start.23 = (bf16[16,128,3,64]{1,3,2,0:T(8,128)(2,1)S(1)}, bf16[16,128,3,64]{1,3,2,0:T(8,128)(2,1)}, u32[]{:S(2)}) copy-start(bf16[16,128,3,64]{1,3,2,0:T(8,128)(2,1)} %get-tuple-element.67) | copy-start | bytes 2359300
  647.6 7.1 copy-start.29
  647.6 8.0 copy-start.32
  654.5 8.7 copy-start.33
  655.6 14.1 %copy-start.11 = (bf16[4096,192]{0,1:T(8,128)(2,1)}, bf16[4096,192]{0,1:T(8,128)(2,1)S(1)}, u32[]{:S(2)}) copy-start(bf16[4096,192]{0,1:T(8,128)(2,1)S(1)} %constant_dynamic-update-slice_fusion.1) | copy-start | bytes 4718596
  661.9 8.9 copy-start.31
  683.6 266.4 %all-reduce.16.cloned.1.call-start = ((), (), s32[]{:S(2)}) async-start(), calls=%async_computation.4 | async-start | bytes 7077888 | tf_op jit(solution)/shard_map/psum | solution.py:235
  683.7 12.1 %copy-start.14 = (bf16[4096,192]{0,1:T(8,128)(2,1)S(1)}, bf16[4096,192]{0,1:T(8,128)(2,1)}, u32[]{:S(2)}) copy-start(bf16[4096,192]{0,1:T(8,128)(2,1)} %copy-done.13) | copy-start | bytes 4718596
  695.8 10.4 %slice-start.5 = ((s8[6291456]{0:T(1024)(128)(4,1)}), s8[4194304]{0:T(1024)(128)(4,1)S(1)}, s32[]{:S(2)}) async-start(s8[6291456]{0:T(1024)(128)(4,1)} %bitcast.145), calls=%async_computation.10 | async-start | bytes 8388608
  695.8 10.4 %copy-start.12 = (bf16[4096,192]{0,1:T(8,128)(2,1)S(1)}, bf16[4096,192]{0,1:T(8,128)(2,1)}, u32[]{:S(2)}) copy-start(bf16[4096,192]{0,1:T(8,128)(2,1)} %copy-done.11) | copy-start | bytes 4718596
  701.0 7.3 slice-start
  701.0 7.3 slice-start.1
  701.0 7.3 copy-start.7
  709.2 7.4 copy-start.42
  709.2 7.4 copy-start.43
  709.2 7.4 copy-start.51
  803.6 159.4 %copy-start.1 = (bf16[768,768]{1,0:T(8,128)(2,1)S(1)}, bf16[768,768]{1,0:T(8,128)(2,1)}, u32[]{:S(2)}) copy-start(bf16[768,768]{1,0:T(8,128)(2,1)} %param.36) | copy-start | bytes 3538948
  (24 other events, 107.9 us)
Sparse Core Ops, SparseCore 0:
  61.2 122.2 all-reduce.7
  241.1 119.7 all-reduce.9
  410.7 119.7 all-reduce.11
  683.8 119.7 all-reduce.13
  808.3 141.6 all-reduce.15
where the time goes:
time: 974 us; the launch traced here: 970 us
  waiting for transfers between devices  525 us (54%)
  matrix products  247 us (25%)
  other arithmetic  106 us (11%)
  local copies, waits for them, and re-layouts  37.7 us (4%)
  blocking collectives  36.9 us (4%)
  between operations  16.5 us (2%)
    psum x1, waiting for transfers between devices, per_device(): lax.psum(grad_query_weight.astype(jnp.bfloat16), 'dp').astype(jnp.float32)  134 us
    psum x1, waiting for transfers between devices, per_device(): lax.psum(row_dot(mixed_heads, output_weight).astype(jnp.bfloat16), 'tensor')  122 us
    psum x1, waiting for transfers between devices, per_device(): lax.psum(row_dot(active, down_weight).astype(jnp.bfloat16), 'tensor')  120 us
    psum x1, waiting for transfers between devices, per_device(): lax.psum(dot_last(grad_inner_low, up_weight).astype(jnp.bfloat16), 'tensor')  104 us
    dot_general x6, matrix products, row_dot(): return jnp.dot(left_side, right_side, preferred_element_type=jnp.float32)  61.6 us
    dot_general x6, matrix products, dot_last(): lax.dot_general(left_side, right_side, (((1,), (1,)), ((), ())), preferre...  48.4 us
    psum x1, waiting for transfers between devices, per_device(): lax.psum((dot_last(low_parts[0], query_weight) + dot_last(low_parts[1], k...  44.8 us
    dot_general x6, matrix products, dot_first(): lax.dot_general(left_side, right_side, (((0,), (0,)), ((), ())), preferre...  41.8 us
  transfers between devices with their start and end apart: 5, of which 5 were waited for; matrix products, arithmetic and copies ran while one was open for 7% of the time, Pallas kernels for 0%

commit v1 on v0

v1 whole, which is shorter than its diff:
```python
import functools

import jax
import jax.numpy as jnp
from jax import lax
from jax.experimental import pallas as pl
from jax.experimental.pallas import tpu as pltpu
from jax.sharding import PartitionSpec as P

HEAD_DIM = 64
SHORT_LEN = 128
LONG_LEN = 512
ROWS = 512
SLOTS = ROWS // SHORT_LEN
PAIR = 2 * HEAD_DIM
MASKED = -30000.0
F32 = jnp.float32
BF16 = jnp.bfloat16
VMEM_LIMIT = 62 * 1024 * 1024


def nn(left, right):
    return lax.dot_general(left, right, (((1,), (0,)), ((), ())), preferred_element_type=F32)


def nt(left, right):
    return lax.dot_general(left, right, (((1,), (1,)), ((), ())), preferred_element_type=F32)


def tn(left, right):
    return lax.dot_general(left, right, (((0,), (0,)), ((), ())), preferred_element_type=F32)


def fold_rows(values):
    return jnp.sum(values.reshape(-1, 8, values.shape[-1]), axis=0)


def total_rows(values):
    return jnp.sum(values, axis=0, keepdims=True)


def half_mask(which):
    lanes = lax.broadcasted_iota(jnp.int32, (1, PAIR), 1)
    return (lanes >= HEAD_DIM) if which else (lanes < HEAD_DIM)


def short_valid(meta, block, slot):
    index = SLOTS * (2 * block + meta[0][0]) + slot
    return jnp.where(index < meta[3][0], meta[1][index], 0)


def long_valid(meta, block, short_blocks):
    index = 2 * (block - short_blocks) + 1 - meta[0][0]
    return jnp.where(index < meta[4][0], meta[2][index], 0)


def norm_rows(values):
    centre = values - jnp.mean(values, axis=-1, keepdims=True)
    scale = lax.rsqrt(jnp.mean(centre * centre, axis=-1, keepdims=True) + 1e-12)
    return centre * scale, scale


def norm_back(incoming, normed, scale, gain):
    grad = incoming * gain
    inner = grad - jnp.mean(grad, axis=-1, keepdims=True)
    inner = inner - normed * jnp.mean(grad * normed, axis=-1, keepdims=True)
    return scale * inner


def load_attention_weights(pieces, wqkv, wout, bias, sems):
    width = wqkv.shape[0] // 12
    copies = []
    for j, piece in enumerate(pieces):
        for k in range(3):
            copies.append(
                (piece.at[pl.ds(k * width, width)], wqkv.at[pl.ds((4 * k + j) * width, width)])
            )
        copies.append((piece.at[pl.ds(3 * width, width)], wout.at[pl.ds(j * width, width)]))
        copies.append((piece.at[pl.ds(4 * width, 16)], bias.at[pl.ds(16 * j, 16)]))
    started = [pltpu.make_async_copy(s, d, sems.at[n]) for n, (s, d) in enumerate(copies)]
    for copy in started:
        copy.start()
    for copy in started:
        copy.wait()


def attention_forward_kernel(
    short_blocks, core, slen, llen, scount, lcount, x, a0, a1, a2, a3, vec,
    qkv, mixed, normed, stat, wqkv, wout, bias, sems,
):
    meta = (core, slen, llen, scount, lcount)
    block = pl.program_id(0)
    width = wout.shape[0]

    @pl.when(block == 0)
    def _():
        load_attention_weights((a0, a1, a2, a3), wqkv, wout, bias, sems)

    low = x[...]
    small = bias[...].astype(F32)
    query_bias = sum(small[16 * j + 1 + j : 16 * j + 2 + j] for j in range(4))
    value_bias = sum(small[16 * j + 5 + j : 16 * j + 6 + j] for j in range(4))
    qkv[:, 0:width] = (nt(low, wqkv[0:width]) + query_bias).astype(BF16)
    qkv[:, width : 2 * width] = nt(low, wqkv[width : 2 * width]).astype(BF16)
    qkv[:, 2 * width : 3 * width] = (nt(low, wqkv[2 * width : 3 * width]) + value_bias).astype(BF16)
    stat[...] = jnp.zeros_like(stat)
    lanes = lax.broadcasted_iota(jnp.int32, (1, 128), 1)

    def one_tile(pair, query_at, queries, key_at, keys, valid):
        column = pl.multiple_of(pair * PAIR, PAIR)
        q = qkv[query_at : query_at + queries, pl.ds(column, PAIR)] * jnp.asarray(0.125, BF16)
        k = qkv[key_at : key_at + keys, pl.ds(width + column, PAIR)]
        v = qkv[key_at : key_at + keys, pl.ds(2 * width + column, PAIR)]
        live = lax.broadcasted_iota(jnp.int32, (1, keys), 1) < valid
        parts = []
        logs = stat[query_at : query_at + queries]
        for e in range(2):
            scores = nt(jnp.where(half_mask(e), q, jnp.zeros_like(q)), k)
            scores = jnp.where(live, scores, MASKED)
            top = jnp.max(scores, axis=-1, keepdims=True)
            weights = jnp.exp(scores - top)
            total = jnp.sum(weights, axis=-1, keepdims=True)
            parts.append(nn(weights.astype(BF16), v) * (1.0 / total))
            logs = jnp.where(lanes == 2 * pair + e, top + jnp.log(total), logs)
        stat[query_at : query_at + queries] = logs
        mixed[query_at : query_at + queries, pl.ds(column, PAIR)] = jnp.where(
            half_mask(0), parts[0], parts[1]
        ).astype(BF16)

    @pl.when(block < short_blocks)
    def _():
        def body(pair, carry):
            for slot in range(SLOTS):
                at = slot * SHORT_LEN
                one_tile(pair, at, SHORT_LEN, at, SHORT_LEN, short_valid(meta, block, slot))
            return carry

        lax.fori_loop(0, width // PAIR, body, 0)

    @pl.when(block >= short_blocks)
    def _():
        valid = long_valid(meta, block, short_blocks)

        def body(pair, carry):
            for part in range(2):
                one_tile(pair, part * 256, 256, 0, LONG_LEN, valid)
            return carry

        lax.fori_loop(0, width // PAIR, body, 0)

    hidden = low.astype(F32) + (nn(mixed[...], wout[...]) + vec[0:1])
    rows, scale = norm_rows(hidden)
    normed[...] = rows.astype(BF16)
    stat[...] = jnp.where(lanes == 12, scale, stat[...])


def ffn_forward_kernel(
    short_blocks, core, slen, llen, scount, lcount, normed, cotangent, u0, u1, u2, u3,
    d0, d1, d2, d3, b0, b1, b2, b3, vec,
    layer_out, grad_low, slope, down_grad, sums, active, down_sum, vec_sum,
):
    meta = (core, slen, llen, scount, lcount)
    block = pl.program_id(0)
    width = u0.shape[1]

    @pl.when(block == 0)
    def _():
        down_sum[...] = jnp.zeros_like(down_sum)
        vec_sum[...] = jnp.zeros_like(vec_sum)

    first = normed[...].astype(F32) * vec[1:2] + vec[2:3]
    first_low = first.astype(BF16)
    total = first + vec[3:4]
    for j, (up, down, bias) in enumerate(((u0, d0, b0), (u1, d1, b1), (u2, d2, b2), (u3, d3, b3))):
        inner = nn(first_low, up[...]) + bias[0:1].astype(F32)
        chance = 0.5 * (1.0 + lax.erf(inner * 0.7071067811865476))
        units = (inner * chance).astype(BF16)
        slope[:, j * width : (j + 1) * width] = (
            chance + inner * jnp.exp(-0.5 * inner * inner) * 0.3989422804014327
        ).astype(BF16)
        if j < 2:
            active[j] = units
        total = total + nn(units, down[...])
    rows, scale = norm_rows(total)
    layer_out[...] = (rows * vec[4:5] + vec[5:6]).astype(BF16)
    position = lax.broadcasted_iota(jnp.int32, (ROWS, 1), 0)
    slot = position // SHORT_LEN
    short_limit = jnp.zeros((ROWS, 1), jnp.int32)
    for n in range(SLOTS):
        short_limit = jnp.where(slot == n, short_valid(meta, jnp.minimum(block, short_blocks - 1), n), short_limit)
    long_limit = long_valid(meta, jnp.maximum(block, short_blocks), short_blocks)
    is_short = block < short_blocks
    alive = jnp.where(is_short, position % SHORT_LEN, position) < jnp.where(
        is_short, short_limit, long_limit
    )
    upstream = jnp.where(alive, cotangent[...].astype(F32), 0.0)
    grad = norm_back(upstream, rows, scale, vec[4:5])
    low = grad.astype(BF16)
    grad_low[...] = low
    vec_sum[0] += fold_rows(upstream * rows)
    vec_sum[1] += fold_rows(upstream)
    vec_sum[2] += fold_rows(grad)
    for j in range(2):
        down_sum[j] += tn(active[j], low)

    @pl.when(block == pl.num_programs(0) - 1)
    def _():
        down_grad[...] = down_sum[...].astype(BF16)
        sums[...] = jnp.zeros_like(sums)
        for n in range(3):
            sums[n : n + 1] = total_rows(vec_sum[n])


def ffn_backward_kernel(
    grad_low, slope, normed, u0, u1, u2, u3, d0, d1, d2, d3, vec,
    first_grad, up_grad, sums, up_sum, vec_sum,
):
    block = pl.program_id(0)
    width = u0.shape[1]

    @pl.when(block == 0)
    def _():
        up_sum[...] = jnp.zeros_like(up_sum)
        vec_sum[...] = jnp.zeros_like(vec_sum)

    low = grad_low[...]
    first_low = (normed[...].astype(F32) * vec[1:2] + vec[2:3]).astype(BF16)
    total = low.astype(F32)
    for j, (up, down) in enumerate(((u0, d0), (u1, d1), (u2, d2), (u3, d3))):
        inner = nt(low, down[...]) * slope[:, j * width : (j + 1) * width].astype(F32)
        inner_low = inner.astype(BF16)
        total = total + nt(inner_low, up[...])
        if j < 2:
            vec_sum[j] += fold_rows(inner)
            up_sum[j] += tn(first_low, inner_low)
    first_grad[...] = total.astype(BF16)

    @pl.when(block == pl.num_programs(0) - 1)
    def _():
        up_grad[...] = up_sum[...].astype(BF16)
        sums[...] = jnp.zeros_like(sums)
        for n in range(2):
            sums[n : n + 1] = total_rows(vec_sum[n])


def attention_backward_kernel(
    short_blocks, core, slen, llen, scount, lcount, first_grad, normed, stat, qkv, mixed, x,
    a0, a1, a2, a3, vec,
    input_grad, out_grad, qkv_grad, sums, wqkv, wout, bias, sems, low_qkv, mixed_grad,
    out_sum, qkv_sum, vec_sum,
):
    meta = (core, slen, llen, scount, lcount)
    block = pl.program_id(0)
    width = wout.shape[0]
    half = width // 2

    @pl.when(block == 0)
    def _():
        load_attention_weights((a0, a1, a2, a3), wqkv, wout, bias, sems)
        out_sum[...] = jnp.zeros_like(out_sum)
        qkv_sum[...] = jnp.zeros_like(qkv_sum)
        vec_sum[...] = jnp.zeros_like(vec_sum)

    incoming = first_grad[...].astype(F32)
    rows = normed[...].astype(F32)
    grad = norm_back(incoming, rows, stat[:, 12:13], vec[1:2])
    low = grad.astype(BF16)
    vec_sum[0] += fold_rows(incoming * rows)
    vec_sum[1] += fold_rows(incoming)
    vec_sum[2] += fold_rows(grad)
    out_sum[...] += tn(mixed[:, 0:half], low)
    mixed_grad[...] = nt(low, wout[...]).astype(BF16)

    def one_tile(pair, at, size, valid):
        column = pl.multiple_of(pair * PAIR, PAIR)
        span = pl.ds(at, size)
        q = qkv[span, pl.ds(column, PAIR)] * jnp.asarray(0.125, BF16)
        k = qkv[span, pl.ds(width + column, PAIR)]
        v = qkv[span, pl.ds(2 * width + column, PAIR)]
        g = mixed_grad[span, pl.ds(column, PAIR)]
        own = g.astype(F32) * mixed[span, pl.ds(column, PAIR)].astype(F32)
        live = lax.broadcasted_iota(jnp.int32, (1, size), 1) < valid
        logs = stat[span]
        lanes = lax.broadcasted_iota(jnp.int32, (1, 128), 1)
        parts = []
        for e in range(2):
            pick = half_mask(e)
            q_e = jnp.where(pick, q, jnp.zeros_like(q))
            g_e = jnp.where(pick, g, jnp.zeros_like(g))
            k_e = jnp.where(pick, k, jnp.zeros_like(k))
            log = jnp.sum(jnp.where(lanes == 2 * pair + e, logs, 0.0), axis=-1, keepdims=True)
            delta = jnp.sum(jnp.where(pick, own, 0.0), axis=-1, keepdims=True)
            probs = jnp.where(live, jnp.exp(nt(q_e, k) - log), 0.0)
            scores = (probs * (nt(g_e, v) - delta)).astype(BF16)
            parts.append((nn(scores, k_e), tn(scores, q_e), tn(probs.astype(BF16), g_e)))
        dq = (parts[0][0] + parts[1][0]) * 0.125
        dk = parts[0][1] + parts[1][1]
        dv = parts[0][2] + parts[1][2]
        low_qkv[span, pl.ds(column, PAIR)] = dq.astype(BF16)
        low_qkv[span, pl.ds(width + column, PAIR)] = dk.astype(BF16)
        low_qkv[span, pl.ds(2 * width + column, PAIR)] = dv.astype(BF16)

    @pl.when(block < short_blocks)
    def _():
        def body(pair, carry):
            for slot in range(SLOTS):
                one_tile(pair, slot * SHORT_LEN, SHORT_LEN, short_valid(meta, block, slot))
            return carry

        lax.fori_loop(0, width // PAIR, body, 0)

    @pl.when(block >= short_blocks)
    def _():
        valid = long_valid(meta, block, short_blocks)

        def body(pair, carry):
            one_tile(pair, 0, LONG_LEN, valid)
            return carry

        lax.fori_loop(0, width // PAIR, body, 0)

    vec_sum[3] += fold_rows(low_qkv[:, 0:width].astype(F32))
    vec_sum[4] += fold_rows(low_qkv[:, 2 * width : 3 * width].astype(F32))
    for k in range(3):
        qkv_sum[k] += tn(low_qkv[:, k * width : k * width + half], x[...])
    input_grad[...] = (grad + nn(low_qkv[...], wqkv[...])).astype(BF16)

    @pl.when(block == pl.num_programs(0) - 1)
    def _():
        out_grad[...] = out_sum[...].astype(BF16)
        qkv_grad[...] = qkv_sum[...].astype(BF16)
        sums[...] = jnp.zeros_like(sums)
        for n in range(5):
            sums[n : n + 1] = total_rows(vec_sum[n])


def const_spec(shape):
    return pl.BlockSpec(
        shape, lambda *_: (0,) * len(shape), pipeline_mode=pl.Buffered(1)
    )


def any_spec():
    return pl.BlockSpec(memory_space=pl.ANY)


def own_spec(width):
    return pl.BlockSpec((ROWS, width), lambda i, *_: (i, 0))


def compute(meta, tokens, cotangent, pieces, ups, downs, vec, short_blocks, long_blocks):
    blocks = short_blocks + long_blocks
    rows = blocks * ROWS
    d = tokens.shape[1]
    width = ups[0].shape[1]
    half = d // 2

    def global_block(i, core, *_):
        return (2 * i + jnp.where(i < short_blocks, core[0], 1 - core[0]), 0)

    global_spec = pl.BlockSpec((ROWS, d), global_block)
    bias_spec = pl.BlockSpec((16, d), lambda *_: (d // 16, 0), pipeline_mode=pl.Buffered(1))
    vec_spec = const_spec((8, d))
    params = pltpu.CompilerParams(
        dimension_semantics=("arbitrary",), vmem_limit_bytes=VMEM_LIMIT
    )
    weights_scratch = [
        pltpu.VMEM((3 * d, d), BF16),
        pltpu.VMEM((d, d), BF16),
        pltpu.VMEM((64, d), BF16),
        pltpu.SemaphoreType.DMA((20,)),
    ]
    sds = jax.ShapeDtypeStruct

    qkv, mixed, normed, stat = pl.pallas_call(
        functools.partial(attention_forward_kernel, short_blocks),
        name="attention_forward",
        grid_spec=pltpu.PrefetchScalarGridSpec(
            num_scalar_prefetch=5,
            grid=(blocks,),
            in_specs=[global_spec] + [any_spec()] * 4 + [vec_spec],
            out_specs=[own_spec(3 * d), own_spec(d), own_spec(d), own_spec(128)],
            scratch_shapes=weights_scratch,
        ),
        out_shape=[sds((rows, 3 * d), BF16), sds((rows, d), BF16), sds((rows, d), BF16), sds((rows, 128), F32)],
        compiler_params=params,
        cost_estimate=pl.CostEstimate(
            flops=2 * rows * d * 4 * d + 4 * rows * 320 * d,
            bytes_accessed=rows * d * 12 + 8 * d * d,
            transcendentals=rows * 320 * 12,
        ),
    )(*meta, tokens, *pieces, vec)

    layer_out, grad_low, slope, down_grad, sums_two = pl.pallas_call(
        functools.partial(ffn_forward_kernel, short_blocks),
        name="ffn_forward",
        grid_spec=pltpu.PrefetchScalarGridSpec(
            num_scalar_prefetch=5,
            grid=(blocks,),
            in_specs=[own_spec(d), global_spec] + [const_spec((d, width))] * 4
            + [const_spec((width, d))] * 4 + [bias_spec] * 4 + [vec_spec],
            out_specs=[own_spec(d), own_spec(d), own_spec(4 * width),
                       const_spec((2, width, d)), const_spec((8, d))],
            scratch_shapes=[pltpu.VMEM((2, ROWS, width), BF16), pltpu.VMEM((2, width, d), F32),
                            pltpu.VMEM((3, 8, d), F32)],
        ),
        out_shape=[sds((rows, d), BF16), sds((rows, d), BF16), sds((rows, 4 * width), BF16),
                   sds((2, width, d), BF16), sds((8, d), F32)],
        compiler_params=params,
        cost_estimate=pl.CostEstimate(
            flops=2 * rows * d * 10 * width, bytes_accessed=rows * d * 20, transcendentals=rows * 8 * width
        ),
    )(*meta, normed, cotangent, *ups, *downs, *pieces, vec)

    first_grad, up_grad, sums_up = pl.pallas_call(
        ffn_backward_kernel,
        name="ffn_backward",
        grid_spec=pltpu.PrefetchScalarGridSpec(
            num_scalar_prefetch=0,
            grid=(blocks,),
            in_specs=[own_spec(d), own_spec(4 * width), own_spec(d)] + [const_spec((d, width))] * 4
            + [const_spec((width, d))] * 4 + [vec_spec],
            out_specs=[own_spec(d), const_spec((2, d, width)), const_spec((8, width))],
            scratch_shapes=[pltpu.VMEM((2, d, width), F32), pltpu.VMEM((2, 8, width), F32)],
        ),
        out_shape=[sds((rows, d), BF16), sds((2, d, width), BF16), sds((8, width), F32)],
        compiler_params=params,
        cost_estimate=pl.CostEstimate(
            flops=2 * rows * d * 10 * width, bytes_accessed=rows * d * 16, transcendentals=0
        ),
    )(grad_low, slope, normed, *ups, *downs, vec)

    input_grad, out_grad, qkv_grad, sums_one = pl.pallas_call(
        functools.partial(attention_backward_kernel, short_blocks),
        name="attention_backward",
        grid_spec=pltpu.PrefetchScalarGridSpec(
            num_scalar_prefetch=5,
            grid=(blocks,),
            in_specs=[own_spec(d), own_spec(d), own_spec(128), own_spec(3 * d), own_spec(d), global_spec]
            + [any_spec()] * 4 + [vec_spec],
            out_specs=[own_spec(d), const_spec((half, d)), const_spec((3, half, d)), const_spec((8, d))],
            scratch_shapes=weights_scratch
            + [pltpu.VMEM((ROWS, 3 * d), BF16), pltpu.VMEM((ROWS, d), BF16), pltpu.VMEM((half, d), F32),
               pltpu.VMEM((3, half, d), F32), pltpu.VMEM((5, 8, d), F32)],
        ),
        out_shape=[sds((rows, d), BF16), sds((half, d), BF16), sds((3, half, d), BF16), sds((8, d), F32)],
        compiler_params=params,
        cost_estimate=pl.CostEstimate(
            flops=2 * rows * d * 6 * d + 10 * rows * 320 * d,
            bytes_accessed=rows * d * 16,
            transcendentals=rows * 320 * 12,
        ),
    )(*meta, first_grad, normed, stat, qkv, mixed, tokens, *pieces, vec)
    return layer_out, input_grad, down_grad, up_grad, out_grad, qkv_grad, sums_two, sums_up, sums_one


def per_device(
    tokens,
    cotangent,
    short_len,
    long_len,
    short_count,
    long_count,
    query_weight,
    query_bias,
    key_weight,
    value_weight,
    value_bias,
    output_weight,
    output_bias,
    first_gain,
    first_shift,
    up_weight,
    up_bias,
    down_weight,
    down_bias,
    second_gain,
    second_shift,
):
    d = tokens.shape[1]
    head_width = query_weight.shape[1]
    short_blocks = short_len.shape[0] * SHORT_LEN // (2 * ROWS)
    long_blocks = long_len.shape[0] * LONG_LEN // (2 * ROWS)
    blocks = short_blocks + long_blocks
    core = lax.axis_index("tensor") % 2
    meta = (core.astype(jnp.int32).reshape(1), short_len, long_len, short_count, long_count)

    def swap(values, bit):
        size = lax.axis_size("tensor")
        return lax.ppermute(values, "tensor", [(i, i ^ bit) for i in range(size)])

    def gather(piece):
        across = swap(piece, 2)
        return (piece, swap(piece, 1), across, swap(across, 1))

    def placed(vector, slot):
        return jnp.pad(vector, (slot * head_width, d - (slot + 1) * head_width))

    biases = jnp.stack(
        [up_bias]
        + [placed(query_bias, j) for j in range(4)]
        + [placed(value_bias, j) for j in range(4)]
        + [jnp.zeros_like(up_bias)] * 7
    )
    piece = jnp.concatenate(
        [query_weight.T, key_weight.T, value_weight.T, output_weight, biases], axis=0
    )
    pieces = gather(piece)
    ups = gather(up_weight)
    downs = gather(down_weight)
    vec = jnp.stack(
        [output_bias, first_gain, first_shift, down_bias, second_gain, second_shift, down_bias, down_bias]
    ).astype(F32)

    out_rows, in_rows, down_grad, up_grad, out_grad, qkv_grad, sums_two, sums_up, sums_one = compute(
        meta, tokens, cotangent, pieces, ups, downs, vec, short_blocks, long_blocks
    )

    def whole_rows(own):
        other = swap(own, 1)
        own = own.reshape(blocks, 1, ROWS, d)
        other = other.reshape(blocks, 1, ROWS, d)
        is_long = (jnp.arange(blocks) >= short_blocks).astype(jnp.int32)
        mine_first = (core == is_long).reshape(blocks, 1, 1, 1)
        lead = jnp.where(mine_first, own, other)
        trail = jnp.where(mine_first, other, own)
        return jnp.concatenate([lead, trail], axis=1).reshape(2 * blocks * ROWS, d)

    layer_output = whole_rows(out_rows)
    input_grad = whole_rows(in_rows).astype(F32)

    def both(mine, partner):
        return (mine.astype(F32) + swap(partner, 1).astype(F32)).astype(BF16)

    def reduced(values):
        return lax.psum(values, "dp")

    grad_down = reduced(both(down_grad[0], down_grad[1])).astype(F32)
    grad_up = reduced(both(up_grad[0], up_grad[1])).astype(F32)
    grad_out = both(out_grad[:head_width], out_grad[head_width:])
    grad_qkv = both(qkv_grad[:, :head_width], qkv_grad[:, head_width:])
    shared = jnp.concatenate([sums_two[0:3], sums_one[0:3]], axis=0)
    shared = (shared + swap(shared, 1)).astype(BF16)
    mine = jnp.concatenate(
        [sums_up[0], sums_one[3, :head_width], sums_one[4, :head_width]]
    )
    partner = jnp.concatenate(
        [sums_up[1], sums_one[3, head_width : 2 * head_width], sums_one[4, head_width : 2 * head_width]]
    )
    split = both(mine, partner)
    small = jnp.concatenate([shared.reshape(-1), split])
    small = jnp.pad(small, (0, 16 * d - small.shape[0])).reshape(16, d)
    last = jnp.concatenate([grad_out, grad_qkv.reshape(3 * head_width, d), small], axis=0)
    last = reduced(last).astype(F32)
    w = head_width
    small = last[4 * w :].reshape(-1)
    grad_up_bias = small[6 * d : 7 * d]
    grad_query_bias = small[7 * d : 7 * d + w]
    grad_value_bias = small[7 * d + w : 7 * d + 2 * w]
    return (
        layer_output,
        input_grad,
        last[w : 2 * w].T,
        grad_query_bias,
        last[2 * w : 3 * w].T,
        last[3 * w : 4 * w].T,
        grad_value_bias,
        last[0:w],
        small[5 * d : 6 * d],
        small[3 * d : 4 * d],
        small[4 * d : 5 * d],
        grad_up,
        grad_up_bias,
        grad_down,
        small[2 * d : 3 * d],
        small[0:d],
        small[d : 2 * d],
    )


def solution(mesh):
    return jax.shard_map(
        per_device,
        mesh=mesh,
        in_specs=(
            P("dp", None),
            P("dp", None),
            P("dp"),
            P("dp"),
            P("dp"),
            P("dp"),
            P(None, "tensor"),
            P("tensor"),
            P(None, "tensor"),
            P(None, "tensor"),
            P("tensor"),
            P("tensor", None),
            P(),
            P(),
            P(),
            P(None, "tensor"),
            P("tensor"),
            P("tensor", None),
            P(),
            P(),
            P(),
        ),
        out_specs=(
            P("dp", None),
            P("dp", None),
            P(None, "tensor"),
            P("tensor"),
            P(None, "tensor"),
            P(None, "tensor"),
            P("tensor"),
            P("tensor", None),
            P(),
            P(),
            P(),
            P(None, "tensor"),
            P("tensor"),
            P("tensor", None),
            P(),
            P(),
            P(),
        ),
        check_vma=False,
    )
```

time: 974 us -> 490 us (0.50)
  waiting for transfers between devices: 525 us -> 193 us
  matrix products: 247 us -> 0 us
  Pallas kernels: 0 us -> 208 us
  other arithmetic: 106 us -> 26 us
  blocking collectives: 36.9 us -> 0 us
    psum x5 -> x1, waiting for transfers between devices: 525 us -> 116 us  [reduced(): return lax.psum(values, 'dp')]
    dot_general x30 -> x0, matrix products: 247 us -> none  [the longest x6 61.6 us: row_dot(): return jnp.dot(left_side, right_side, preferred_element_type=jnp.float32)]
    pallas_call x0 -> x4, Pallas kernels: none -> 208 us  [the longest x1 70.1 us: compute(): pl.pallas_call(functools.partial(attention_backward_kernel, short_blocks)...]
    ppermute x0 -> x17, waiting for transfers between devices: none -> 76.3 us  [swap(): return lax.ppermute(values, 'tensor', [(i, i ^ bit) for i in range(size)])]
    reduce_sum x13 -> x0, other arithmetic: 64.6 us -> none  [the longest x2 22.1 us: norm_backward(): jnp.sum(incoming * normed, axis=0)]
    psum x1 -> x0, blocking collectives: 36.9 us -> none  [per_device(): lax.psum(grad_query_bias.astype(jnp.bfloat16), 'dp').astype(jnp.float32)]
    unnamed x147 -> x32, local copies, waits for them, and re-layouts: 18 us -> 1.08 us
    add x3 -> x0, other arithmetic: 12.7 us -> none  [the longest x1 12.7 us: per_device(): input_grad = grad_hidden + input_total]
  transfers between devices with their start and end apart: 5 -> 18, of which waited for: 5 -> 5; matrix products, arithmetic and copies ran while one was open for 7% -> 9% of each run, Pallas kernels for 0% -> 12%
where the time goes in v1:
time: 490 us; the launch traced here: 489 us
  Pallas kernels  208 us (42%)
  waiting for transfers between devices  193 us (39%)
  local copies, waits for them, and re-layouts  38.6 us (8%)
  other arithmetic  26 us (5%)
  between operations  15.8 us (3%)
  starting transfers between devices  8.29 us (2%)
    psum x1, waiting for transfers between devices, reduced(): return lax.psum(values, 'dp')  116 us
    ppermute x17, waiting for transfers between devices, swap(): return lax.ppermute(values, 'tensor', [(i, i ^ bit) for i in range(size)])  76.3 us
    pallas_call x1, Pallas kernels, compute(): pl.pallas_call(functools.partial(attention_backward_kernel, short_blocks)...  70.1 us
    pallas_call x1, Pallas kernels, compute(): pl.pallas_call(functools.partial(attention_forward_kernel, short_blocks),...  60.6 us
    pallas_call x1, Pallas kernels, compute(): pl.pallas_call(functools.partial(ffn_forward_kernel, short_blocks), name=...  42.5 us
    pallas_call x1, Pallas kernels, compute(): pl.pallas_call(ffn_backward_kernel, name='ffn_backward', grid_spec=pltpu....  34.4 us
    convert_element_type x1, local copies, waits for them, and re-layouts, per_device(): input_grad = whole_rows(in_rows).astype(F32)  10.3 us
  transfers between devices with their start and end apart: 18, of which 5 were waited for; matrix products, arithmetic and copies ran while one was open for 9% of the time, Pallas kernels for 12%

profile of v1, /device:TPU:0, one launch (start us, length us, event | category | flops | bytes accessed | tf_op | source)
XLA Modules:
  0.0 488.8 jit_solution(6897798988371418707)
XLA Ops:
  7.3 0.9 fusion.8
  8.3 0.7 stack.50
  9.0 7.3 %concatenate.32.a0.b0 = bf16[784,768]{1,0:T(8,128)(2,1)S(1)} concatenate(bf16[192,768]{1,0:T(8,128)(2,1)} %bitcast.36, bf16[192,768]{1,0:T(8,128)(2,1)} %bitcast.37, bf16[192,768]{1,0:T(8,128)(2,1)} %bitcast.38, bf16[192,768]{1,0:T(8,128)(2,1)} %param.32, bf16[1,768]{1,0:T(2,128)(2,1)S(1)} %stack.50, bf16[1,768]{1,0:T(2,128)(2,1)S(1)} %stack.51, bf16[1,768]{1,0:T(2,128)(2,1)S(1)} %stack.52, ...), dimensions={0} | concatenate | bytes 2408448 | tf_op jit(solution)/shard_map/concatenate | solution.py:505
  16.3 3.0 collective-permute-start.1
  19.4 0.2 collective-permute-start.4
  19.5 1.9 collective-permute-start.7
  21.4 25.3 %collective-permute-done.1.a2.b2 = bf16[784,768]{1,0:T(8,128)(2,1)S(1)} collective-permute-done((bf16[784,768]{1,0:T(8,128)(2,1)S(1)}, bf16[784,768]{1,0:T(8,128)(2,1)S(1)}, u32[]{:S(2)}, u32[]{:S(2)}) %collective-permute-start.1) | collective-permute-done | bytes 1204256 | tf_op jit(solution)/shard_map/ppermute | solution.py:490
  46.7 0.5 collective-permute-start.3
  47.2 24.9 %collective-permute-done.4.u2 = bf16[768,768]{1,0:T(8,128)(2,1)} collective-permute-done((bf16[768,768]{1,0:T(8,128)(2,1)}, bf16[768,768]{1,0:T(8,128)(2,1)}, u32[]{:S(2)}, u32[]{:S(2)}) %collective-permute-start.4) | collective-permute-done | bytes 1179680 | tf_op jit(solution)/shard_map/ppermute | solution.py:490
  72.1 24.4 %collective-permute-done.7.d2 = bf16[768,768]{1,0:T(8,128)(2,1)} collective-permute-done((bf16[768,768]{1,0:T(8,128)(2,1)}, bf16[768,768]{1,0:T(8,128)(2,1)}, u32[]{:S(2)}, u32[]{:S(2)}) %collective-permute-start.7) | collective-permute-done | bytes 1179680 | tf_op jit(solution)/shard_map/ppermute | solution.py:490
  96.5 1.0 copy-done.15
  97.6 0.5 collective-permute-start.8
  98.2 0.6 convert_element_type.89.vec
  100.2 60.6 %attention_forward.1 = (bf16[2048,2304]{1,0:T(8,128)(2,1)}, bf16[2048,768]{1,0:T(8,128)(2,1)}, bf16[2048,768]{1,0:T(8,128)(2,1)}, f32[2048,128]{1,0:T(8,128)}) custom-call(s32[1]{0:T(128)} %bitcast.core, s32[16]{0:T(128)} %slen.5, s32[4]{0:T(128)} %llen.5, s32[1]{0:T(128)S(6)} %copy.43.scount, s32[1]{0:T(128)S(6)} %copy.44.lcount, bf16[4096,768]{1,0:T(8,128)(2,1)} %x.21, ...), custom_call_target="tpu_custom_call" | custom-call | flops 11676942336 | bytes 23592960 | tf_op jit(solution)/shard_map/attention_forward/pallas_call | solution.py:375
  160.8 42.5 %ffn_forward.1 = (bf16[2048,768]{1,0:T(8,128)(2,1)}, bf16[2048,768]{1,0:T(8,128)(2,1)}, bf16[2048,3072]{1,0:T(8,128)(2,1)}, bf16[2,768,768]{2,1,0:T(8,128)(2,1)}, f32[8,768]{1,0:T(8,128)}) custom-call(s32[1]{0:T(128)} %bitcast.core, s32[16]{0:T(128)} %slen.5, s32[4]{0:T(128)} %llen.5, s32[1]{0:T(128)S(6)} %copy.43.scount, s32[1]{0:T(128)S(6)} %copy.44.lcount, ...), custom_call_target="tpu_custom_call" | custom-call | flops 24159191040 | bytes 31457280 | tf_op jit(solution)/shard_map/ffn_forward/pallas_call | solution.py:394
  203.3 34.4 %ffn_backward.1 = (bf16[2048,768]{1,0:T(8,128)(2,1)}, bf16[2,768,768]{2,1,0:T(8,128)(2,1)}, f32[8,768]{1,0:T(8,128)}) custom-call(bf16[2048,768]{1,0:T(8,128)(2,1)} %get-tuple-element.35.grad_low, bf16[2048,3072]{1,0:T(8,128)(2,1)} %get-tuple-element.36.slope, bf16[2048,768]{1,0:T(8,128)(2,1)} %get-tuple-element.33.normed, bf16[768,768]{1,0:T(8,128)(2,1)} %u0.3, ...), custom_call_target="tpu_custom_call" | custom-call | flops 24159191040 | bytes 25165824 | tf_op jit(solution)/shard_map/ffn_backward/pallas_call | solution.py:415
  237.7 70.1 %attention_backward.1 = (bf16[2048,768]{1,0:T(8,128)(2,1)}, bf16[384,768]{1,0:T(8,128)(2,1)}, bf16[3,384,768]{2,1,0:T(8,128)(2,1)}, f32[8,768]{1,0:T(8,128)}) custom-call(s32[1]{0:T(128)} %bitcast.core, s32[16]{0:T(128)} %slen.5, s32[4]{0:T(128)} %llen.5, s32[1]{0:T(128)S(6)} %copy.43.scount, s32[1]{0:T(128)S(6)} %copy.44.lcount, ...), custom_call_target="tpu_custom_call" | custom-call | flops 19528679424 | bytes 25165824 | tf_op jit(solution)/shard_map/attention_backward/pallas_call | solution.py:433
  307.8 0.7 slice.123
  308.5 0.9 fusion.7
  309.4 1.7 slice.119
  311.2 2.2 slice.121
  313.4 0.4 collective-permute-start.12
  313.8 0.2 collective-permute-start.13
  314.0 0.8 slice_reduce_fusion.7
  314.9 0.4 collective-permute-start.14
  315.3 2.5 slice_bitcast_fusion.1
  317.9 2.5 slice_bitcast_fusion
  320.5 0.4 collective-permute-start.16
  321.1 0.4 collective-permute-start.9
  321.6 1.0 add_convert_fusion.1
  322.6 1.8 add_convert_fusion
  324.4 1.2 pad_maximum_fusion.1
  325.6 2.8 fusion.1
  328.4 2.6 fusion
  331.0 1.6 collective-permute-done.10
  332.7 5.4 %broadcast_select_fusion.1 = (bf16[4,1,512,768]{3,2,0,1:T(8,128)(2,1)S(1)}, bf16[4,1,512,768]{3,2,0,1:T(8,128)(2,1)S(1)}, bf16[4,1,512,768]{3,2,0,1:T(8,128)(2,1)S(1)}, bf16[4,1,512,768]{3,2,0,1:T(8,128)(2,1)S(1)}) fusion(bf16[4,1,512,768]{3,2,0,1:T(8,128)(2,1)} %bitcast.35, bf16[4,1,512,768]{3,2,0,1:T(8,128)(2,1)} %bitcast.8, pred[4]{0:T(512)(128)(4,1)S(1)} %fusion.5, ...), kind=kLoop, calls=%fused_computation.3 | loop fusion | flops 6291456 | bytes 25165828 | tf_op jit(solution)/shard_map/jit(_where)/select_n | solution.py:525
  338.1 5.3 %maximum_convert_fusion = f32[4,2,512,768]{3,2,0,1:T(8,128)} fusion(bf16[4,1,512,768]{3,2,0,1:T(8,128)(2,1)S(1)} %get-tuple-element.62, bf16[4,1,512,768]{3,2,0,1:T(8,128)(2,1)S(1)} %get-tuple-element.61), kind=kLoop, calls=%fused_computation.1 | loop fusion | flops 6291456 | bytes 18874368 | tf_op jit(solution)/shard_map/convert_element_type | solution.py:530
  343.5 10.3 %copy.39 = f32[4,2,512,768]{3,2,1,0:T(8,128)} copy(f32[4,2,512,768]{3,2,0,1:T(8,128)} %maximum_convert_fusion) | data formatting | bytes 25165824 | tf_op jit(solution)/shard_map/convert_element_type | solution.py:530
  353.8 0.6 pad_maximum_fusion
  354.4 3.2 copy.38
  357.6 116.4 %all-reduce.12.cloned.1.call-done = (bf16[784,768]{1,0:T(8,128)(2,1)}, bf16[768,768]{1,0:T(8,128)(2,1)}, bf16[768,768]{1,0:T(8,128)(2,1)}) async-done(((bf16[784,768]{1,0:T(8,128)(2,1)}, bf16[768,768]{1,0:T(8,128)(2,1)}, bf16[768,768]{1,0:T(8,128)(2,1)}), (bf16[784,768]{1,0:T(8,128)(2,1)}, bf16[768,768]{1,0:T(8,128)(2,1)}, bf16[768,768]{1,0:T(8,128)(2,1)})) %all-reduce.12.cloned.1.call-update) | async-done | bytes 3563536 | tf_op jit(solution)/shard_map/psum | solution.py:536
  473.9 1.4 convert_element_type.100
  475.4 1.2 slice_bitcast_fusion.2
  476.7 0.7 slice_reduce_fusion
  477.3 0.9 slice.161
  478.2 1.6 convert_element_type.105
  479.8 1.6 convert_element_type.110
  481.3 0.6 fusion.6
  (83 shorter events, 1.0 us)
Async XLA Ops:
  7.2 90.9 %copy-start.8 = (bf16[768]{0:T(1024)(128)(2,1)S(1)}, bf16[768]{0:T(1024)(128)(2,1)}, u32[]{:S(2)}) copy-start(bf16[768]{0:T(1024)(128)(2,1)} %param.33) | copy-start | bytes 4612
  7.2 90.9 %copy-start.9 = (bf16[768]{0:T(1024)(128)(2,1)S(1)}, bf16[768]{0:T(1024)(128)(2,1)}, u32[]{:S(2)}) copy-start(bf16[768]{0:T(1024)(128)(2,1)} %param.34) | copy-start | bytes 4612
  7.2 90.9 %copy-start.10 = (bf16[768]{0:T(1024)(128)(2,1)S(1)}, bf16[768]{0:T(1024)(128)(2,1)}, u32[]{:S(2)}) copy-start(bf16[768]{0:T(1024)(128)(2,1)} %param.35) | copy-start | bytes 4612
  7.2 90.9 %copy-start.11 = (bf16[768]{0:T(1024)(128)(2,1)S(1)}, bf16[768]{0:T(1024)(128)(2,1)}, u32[]{:S(2)}) copy-start(bf16[768]{0:T(1024)(128)(2,1)} %param.39) | copy-start | bytes 4612
  7.2 90.9 %copy-start.12 = (bf16[768]{0:T(1024)(128)(2,1)S(1)}, bf16[768]{0:T(1024)(128)(2,1)}, u32[]{:S(2)}) copy-start(bf16[768]{0:T(1024)(128)(2,1)} %param.40) | copy-start | bytes 4612
  7.2 90.9 %copy-start.13 = (bf16[768]{0:T(1024)(128)(2,1)S(1)}, bf16[768]{0:T(1024)(128)(2,1)}, u32[]{:S(2)}) copy-start(bf16[768]{0:T(1024)(128)(2,1)} %param.41) | copy-start | bytes 4612
  7.3 466.7 %all-reduce.12.cloned.1.call-start = ((), (), s32[]{:S(2)}) async-start(), calls=%async_computation | async-start | bytes 7127040 | tf_op jit(solution)/shard_map/psum | solution.py:536
  16.3 83.8 %copy-start.4 = (bf16[784,768]{1,0:T(8,128)(2,1)}, bf16[784,768]{1,0:T(8,128)(2,1)S(1)}, u32[]{:S(2)}) copy-start(bf16[784,768]{1,0:T(8,128)(2,1)S(1)} %concatenate.32.a0.b0) | copy-start | bytes 3612676
  16.3 30.4 %collective-permute-start.1 = (bf16[784,768]{1,0:T(8,128)(2,1)S(1)}, bf16[784,768]{1,0:T(8,128)(2,1)S(1)}, u32[]{:S(2)}, u32[]{:S(2)}) collective-permute-start(bf16[784,768]{1,0:T(8,128)(2,1)S(1)} %concatenate.32.a0.b0), channel_id=1, source_target_pairs={{0,2},{1,3},{2,0},{3,1},{4,6},{5,7},{6,4},{7,5},{8,10},{9,11},{10,... | collective-permute-start | bytes 3612680 | tf_op jit(solution)/shard_map/ppermute | solution.py:490
  19.4 77.2 %collective-permute-start = (bf16[784,768]{1,0:T(8,128)(2,1)S(1)}, bf16[784,768]{1,0:T(8,128)(2,1)S(1)}, u32[]{:S(2)}, u32[]{:S(2)}) collective-permute-start(bf16[784,768]{1,0:T(8,128)(2,1)S(1)} %concatenate.32.a0.b0), channel_id=1, source_target_pairs={{0,1},{1,0},{2,3},{3,2},{4,5},{5,4},{6,7},{7,6},{8,9},{9,8},{10,11... | collective-permute-start | bytes 3612680 | tf_op jit(solution)/shard_map/ppermute | solution.py:490
  19.4 52.7 %collective-permute-start.4 = (bf16[768,768]{1,0:T(8,128)(2,1)}, bf16[768,768]{1,0:T(8,128)(2,1)}, u32[]{:S(2)}, u32[]{:S(2)}) collective-permute-start(bf16[768,768]{1,0:T(8,128)(2,1)} %u0.3), channel_id=1, source_target_pairs={{0,2},{1,3},{2,0},{3,1},{4,6},{5,7},{6,4},{7,5},{8,10},{9,11},{10,... | collective-permute-start | bytes 3538952 | tf_op jit(solution)/shard_map/ppermute | solution.py:490
  19.5 77.0 %collective-permute-start.7 = (bf16[768,768]{1,0:T(8,128)(2,1)}, bf16[768,768]{1,0:T(8,128)(2,1)}, u32[]{:S(2)}, u32[]{:S(2)}) collective-permute-start(bf16[768,768]{1,0:T(8,128)(2,1)} %d0.3), channel_id=1, source_target_pairs={{0,2},{1,3},{2,0},{3,1},{4,6},{5,7},{6,4},{7,5},{8,10},{9,11},{10,... | collective-permute-start | bytes 3538952 | tf_op jit(solution)/shard_map/ppermute | solution.py:490
  46.7 52.2 %copy-start.14 = (bf16[784,768]{1,0:T(8,128)(2,1)}, bf16[784,768]{1,0:T(8,128)(2,1)S(1)}, u32[]{:S(2)}) copy-start(bf16[784,768]{1,0:T(8,128)(2,1)S(1)} %collective-permute-done.1.a2.b2) | copy-start | bytes 3612676
  46.7 53.5 %collective-permute-start.2 = (bf16[784,768]{1,0:T(8,128)(2,1)S(1)}, bf16[784,768]{1,0:T(8,128)(2,1)}, u32[]{:S(2)}, u32[]{:S(2)}) collective-permute-start(bf16[784,768]{1,0:T(8,128)(2,1)S(1)} %collective-permute-done.1.a2.b2), channel_id=1, source_target_pairs={{0,1},{1,0},{2,3},{3,2},{4,5},{5,4},{6,7},{7,6},{8,9},{9,8},{10,11... | collective-permute-start | bytes 3612680 | tf_op jit(solution)/shard_map/ppermute | solution.py:490
  46.7 114.1 %collective-permute-start.3 = (bf16[768,768]{1,0:T(8,128)(2,1)}, bf16[768,768]{1,0:T(8,128)(2,1)}, u32[]{:S(2)}, u32[]{:S(2)}) collective-permute-start(bf16[768,768]{1,0:T(8,128)(2,1)} %u0.3), channel_id=1, source_target_pairs={{0,1},{1,0},{2,3},{3,2},{4,5},{5,4},{6,7},{7,6},{8,9},{9,8},{10,11... | collective-permute-start | bytes 3538952 | tf_op jit(solution)/shard_map/ppermute | solution.py:490
  72.1 88.7 %collective-permute-start.6 = (bf16[768,768]{1,0:T(8,128)(2,1)}, bf16[768,768]{1,0:T(8,128)(2,1)}, u32[]{:S(2)}, u32[]{:S(2)}) collective-permute-start(bf16[768,768]{1,0:T(8,128)(2,1)} %d0.3), channel_id=1, source_target_pairs={{0,1},{1,0},{2,3},{3,2},{4,5},{5,4},{6,7},{7,6},{8,9},{9,8},{10,11... | collective-permute-start | bytes 3538952 | tf_op jit(solution)/shard_map/ppermute | solution.py:490
  96.5 64.2 %collective-permute-start.5 = (bf16[768,768]{1,0:T(8,128)(2,1)}, bf16[768,768]{1,0:T(8,128)(2,1)}, u32[]{:S(2)}, u32[]{:S(2)}) collective-permute-start(bf16[768,768]{1,0:T(8,128)(2,1)} %collective-permute-done.4.u2), channel_id=1, source_target_pairs={{0,1},{1,0},{2,3},{3,2},{4,5},{5,4},{6,7},{7,6},{8,9},{9,8},{10,11... | collective-permute-start | bytes 3538952 | tf_op jit(solution)/shard_map/ppermute | solution.py:490
  96.5 1.0 copy-start.15
  97.6 63.2 %collective-permute-start.8 = (bf16[768,768]{1,0:T(8,128)(2,1)}, bf16[768,768]{1,0:T(8,128)(2,1)}, u32[]{:S(2)}, u32[]{:S(2)}) collective-permute-start(bf16[768,768]{1,0:T(8,128)(2,1)} %collective-permute-done.7.d2), channel_id=1, source_target_pairs={{0,1},{1,0},{2,3},{3,2},{4,5},{5,4},{6,7},{7,6},{8,9},{9,8},{10,11... | collective-permute-start | bytes 3538952 | tf_op jit(solution)/shard_map/ppermute | solution.py:490
  307.7 6.1 %copy-start.7 = (f32[8,768]{1,0:T(8,128)S(1)}, f32[8,768]{1,0:T(8,128)}, u32[]{:S(2)}) copy-start(f32[8,768]{1,0:T(8,128)} %get-tuple-element.44) | copy-start | bytes 73732
  311.1 10.0 %collective-permute-start.11 = (bf16[192,768]{1,0:T(8,128)(2,1)}, bf16[192,768]{1,0:T(8,128)(2,1)S(1)}, u32[]{:S(2)}, u32[]{:S(2)}) collective-permute-start(bf16[192,768]{1,0:T(8,128)(2,1)} %slice.119), channel_id=1, source_target_pairs={{0,1},{1,0},{2,3},{3,2},{4,5},{5,4},{6,7},{7,6},{8,9},{9,8},{10,11... | collective-permute-start | bytes 884744 | tf_op jit(solution)/shard_map/ppermute | solution.py:490
  313.4 9.2 %collective-permute-start.12 = (bf16[3,192,768]{2,1,0:T(8,128)(2,1)}, bf16[3,192,768]{2,1,0:T(8,128)(2,1)}, u32[]{:S(2)}, u32[]{:S(2)}) collective-permute-start(bf16[3,192,768]{2,1,0:T(8,128)(2,1)} %slice.121), channel_id=1, source_target_pairs={{0,1},{1,0},{2,3},{3,2},{4,5},{5,4},{6,7},{7,6},{8,9},{9,8},{10,11... | collective-permute-start | bytes 2654216 | tf_op jit(solution)/shard_map/ppermute | solution.py:490
  313.8 7.1 %collective-permute-start.13 = (f32[6,768]{1,0:T(8,128)S(1)}, f32[6,768]{1,0:T(8,128)S(1)}, u32[]{:S(2)}, u32[]{:S(2)}) collective-permute-start(f32[6,768]{1,0:T(8,128)S(1)} %pad_maximum_fusion.2), channel_id=1, source_target_pairs={{0,1},{1,0},{2,3},{3,2},{4,5},{5,4},{6,7},{7,6},{8,9},{9,8},{10,11... | collective-permute-start | bytes 55304 | tf_op jit(solution)/shard_map/ppermute | solution.py:490
  314.9 5.6 %collective-permute-start.14 = (f32[1152]{0:T(1024)S(1)}, f32[1152]{0:T(1024)S(1)}, u32[]{:S(2)}, u32[]{:S(2)}) collective-permute-start(f32[1152]{0:T(1024)S(1)} %concatenate.37), channel_id=1, source_target_pairs={{0,1},{1,0},{2,3},{3,2},{4,5},{5,4},{6,7},{7,6},{8,9},{9,8},{10,11... | collective-permute-start | bytes 13832 | tf_op jit(solution)/shard_map/ppermute | solution.py:490
  315.3 5.8 %copy-start = (bf16[2048,768]{1,0:T(8,128)(2,1)S(1)}, bf16[2048,768]{1,0:T(8,128)(2,1)}, u32[]{:S(2)}) copy-start(bf16[2048,768]{1,0:T(8,128)(2,1)} %get-tuple-element.34) | copy-start | bytes 9437188
  317.8 7.8 %collective-permute-start.15 = (bf16[768,768]{1,0:T(8,128)(2,1)}, bf16[768,768]{1,0:T(8,128)(2,1)}, u32[]{:S(2)}, u32[]{:S(2)}) collective-permute-start(bf16[768,768]{1,0:T(8,128)(2,1)} %slice_bitcast_fusion.1), channel_id=1, source_target_pairs={{0,1},{1,0},{2,3},{3,2},{4,5},{5,4},{6,7},{7,6},{8,9},{9,8},{10,11... | collective-permute-start | bytes 3538952 | tf_op jit(solution)/shard_map/ppermute | solution.py:490
  320.5 7.9 %collective-permute-start.16 = (bf16[768,768]{1,0:T(8,128)(2,1)}, bf16[768,768]{1,0:T(8,128)(2,1)}, u32[]{:S(2)}, u32[]{:S(2)}) collective-permute-start(bf16[768,768]{1,0:T(8,128)(2,1)} %slice_bitcast_fusion), channel_id=1, source_target_pairs={{0,1},{1,0},{2,3},{3,2},{4,5},{5,4},{6,7},{7,6},{8,9},{9,8},{10,11... | collective-permute-start | bytes 3538952 | tf_op jit(solution)/shard_map/ppermute | solution.py:490
  320.9 11.8 %collective-permute-start.10 = (bf16[2048,768]{1,0:T(8,128)(2,1)}, bf16[2048,768]{1,0:T(8,128)(2,1)}, u32[]{:S(2)}, u32[]{:S(2)}) collective-permute-start(bf16[2048,768]{1,0:T(8,128)(2,1)} %get-tuple-element.41), channel_id=1, source_target_pairs={{0,1},{1,0},{2,3},{3,2},{4,5},{5,4},{6,7},{7,6},{8,9},{9,8},{10,11... | collective-permute-start | bytes 9437192 | tf_op jit(solution)/shard_map/ppermute | solution.py:490
  321.1 11.5 %collective-permute-start.9 = (bf16[2048,768]{1,0:T(8,128)(2,1)S(1)}, bf16[2048,768]{1,0:T(8,128)(2,1)}, u32[]{:S(2)}, u32[]{:S(2)}) collective-permute-start(bf16[2048,768]{1,0:T(8,128)(2,1)S(1)} %copy-done), channel_id=1, source_target_pairs={{0,1},{1,0},{2,3},{3,2},{4,5},{5,4},{6,7},{7,6},{8,9},{9,8},{10,11... | collective-permute-start | bytes 9437192 | tf_op jit(solution)/shard_map/ppermute | solution.py:490
  322.6 3.0 copy-start.3
  325.6 2.8 copy-start.2
  475.4 1.9 copy-start.1
  475.4 2.8 copy-start.6
  477.3 2.4 copy-start.5
Sparse Core Ops, SparseCore 0:
  331.1 142.7 all-reduce.11
